TPU v7x, 256 devices: a whole 4x4x8 slice. The times are simulated.
256 devices in a mesh: layer: 8 (over z_lo, y), cell: 32 (over z_hi, x, core).
Axes of the slice: x: 4, y: 4, z: 8 (z_hi: 4, z_lo: 2; z = z_hi * 2 + z_lo), core: 2. Of those that a mesh axis runs over, the one named last changes fastest.
Arguments:
- shower_state: float32 [2, 48, 1024], P(None, 'layer', 'cell'), may hold values from -6 to 6
- cell_valid: int32 [1024], replicated, may hold values 0 or 1
- layer_valid: int32 [48], replicated, may hold values 0 or 1
- energy_bin: int32 [2], replicated, may hold values from 0 to 63
- time_index: int32 [1], replicated, may hold values from 0 to 999
- embed_weight: float32 [512], replicated, may hold values from -6 to 6
- cell_embed: float32 [1024, 512], P('cell'), may hold values from -6 to 6
- layer_embed: float32 [48, 512], P('layer'), may hold values from -6 to 6
- energy_table: float32 [64, 512], replicated, may hold values from -6 to 6
- gain_cells: float32 [512], replicated, may hold values from 0.1 to 1.9
- cell_heads: bfloat16 [512, 1536], replicated, may hold values from -0.25 to 0.25
- cell_merge: bfloat16 [512, 512], replicated, may hold values from -0.25 to 0.25
- cell_scale: float32 [8], replicated, may hold values from 0.5 to 40
- gain_layers: float32 [512], replicated, may hold values from 0.1 to 1.9
- layer_heads: bfloat16 [512, 1536], replicated, may hold values from -0.25 to 0.25
- layer_merge: bfloat16 [512, 512], replicated, may hold values from -0.25 to 0.25
- layer_scale: float32 [8], replicated, may hold values from 0.5 to 40
- gain_expand: float32 [512], replicated, may hold values from 0.1 to 1.9
- expand_weight: bfloat16 [512, 2048], replicated, may hold values from -0.25 to 0.25
- reduce_weight: bfloat16 [2048, 512], replicated, may hold values from -0.125 to 0.125
- gain_final: float32 [512], replicated, may hold values from 0.1 to 1.9
- velocity_head: float32 [512], replicated, may hold values from -0.25 to 0.25
Outputs:
- velocity: float32 [2, 48, 1024], P(None, 'layer', 'cell')
- next_state: float32 [2, 48, 1024], P(None, 'layer', 'cell')
All inputs are finite; a program needn't handle non-finite values.
Results may differ from a plain program's by a relative error of at most 0.018.
The roundings to bfloat16 on the way count: a program that leaves them out, or rounds other values in their place, can miss the bound.
Values may be sent and summed in bfloat16 or wider, within the bound.
A program may use at most 192 MiB of HBM per device.

v0:
```python
import math
import jax
import jax.numpy as jnp
from jax import lax
from jax.sharding import PartitionSpec as P

D = 512
HEADS = 8
HDIM = 64
NBINS = 64
GRID = 1000
STEPS = 2
EPS = 1e-06


def normalize(hidden, gain):
    return hidden * lax.rsqrt(jnp.mean(hidden * hidden, -1, keepdims=True) + EPS) * gain


def head_norm(values):
    split = values.reshape(values.shape[:-1] + (HEADS, HDIM))
    return split * lax.rsqrt(jnp.mean(split * split, -1, keepdims=True) + EPS)


def split_heads(values):
    return values.reshape(values.shape[:-1] + (HEADS, HDIM)).astype(jnp.bfloat16)


def condition(energy_bin, time_index, energy_table):
    onehot = (jnp.arange(NBINS)[None, :] == energy_bin[:, None])[:, :, None]
    picked = jnp.sum(jnp.where(onehot, energy_table[None], 0.0), 1)
    moment = time_index[0].astype(jnp.float32) / GRID
    freqs = jnp.exp(-math.log(1000.0) * jnp.arange(D // 2).astype(jnp.float32) / (D // 2))
    angles = moment * 100.0 * freqs
    return picked + jnp.concatenate([jnp.sin(angles), jnp.cos(angles)])[None]


def online(carry, scores, allowed, values, form):
    top, total, accum = carry
    scores = jnp.where(allowed, scores, -1e30)
    new_top = jnp.maximum(top, jnp.max(scores, -1))
    weights = jnp.where(allowed, jnp.exp(scores - new_top[..., None]), 0.0)
    total = jnp.sum(weights, -1)
    accum = jnp.einsum(
        form, weights.astype(jnp.bfloat16), values, preferred_element_type=jnp.float32
    )
    return (new_top, total, accum)


def on_device(
    shower_state,
    cell_valid,
    layer_valid,
    energy_bin,
    time_index,
    embed_weight,
    cell_embed,
    layer_embed,
    energy_table,
    gain_cells,
    cell_heads,
    cell_merge,
    cell_scale,
    gain_layers,
    layer_heads,
    layer_merge,
    layer_scale,
    gain_expand,
    expand_weight,
    reduce_weight,
    gain_final,
    velocity_head,
):
    shw_count, lay_count, cell_count = shower_state.shape
    width = embed_weight.shape[0]
    cell_first = lax.axis_index("cell") * cell_count
    layer_first = lax.axis_index("layer") * lay_count
    cell_ok = lax.dynamic_slice_in_dim(cell_valid, cell_first, cell_count) == 1
    layer_ok = lax.dynamic_slice_in_dim(layer_valid, layer_first, lay_count) == 1
    cond = condition(energy_bin, time_index, energy_table)
    hidden = (
        shower_state[..., None] * embed_weight
        + cell_embed[None, None]
        + layer_embed[None, :, None]
        + cond[:, None, None]
    )
    normed = normalize(hidden, gain_cells).astype(jnp.bfloat16)
    query_ids = cell_first + jnp.arange(cell_count)
    cell_factor = cell_scale / math.sqrt(HDIM)
    start_cells = (
        jnp.full((shw_count, lay_count, HEADS, cell_count), -1e30, jnp.float32),
        jnp.zeros((shw_count, lay_count, HEADS, cell_count), jnp.float32),
        jnp.zeros((shw_count, lay_count, HEADS, cell_count, HDIM), jnp.float32),
    )
    queries = head_norm(
        jnp.dot(normed, cell_heads[:, :width], preferred_element_type=jnp.float32)
    ).astype(jnp.bfloat16)
    proj = jnp.dot(
        lax.all_gather(normed, "cell", axis=2, tiled=True),
        cell_heads[:, width:],
        preferred_element_type=jnp.float32,
    )
    keys = head_norm(proj[..., :width]).astype(jnp.bfloat16)
    values = split_heads(proj[..., width:])
    count = keys.shape[2]
    scores = (
        jnp.einsum("slqhd,slkhd->slhqk", queries, keys, preferred_element_type=jnp.float32)
        * cell_factor[None, None, :, None, None]
    )
    key_ok = cell_valid == 1
    allowed = key_ok[None, :] | (jnp.arange(count)[None, :] == query_ids[:, None])
    carry = online(start_cells, scores, allowed[None, None, None], values, "slhqk,slkhd->slhqd")
    result = carry[2] / carry[1][..., None]
    mixed = (
        jnp.transpose(result, (0, 1, 3, 2, 4))
        .reshape(shw_count, lay_count, cell_count, width)
        .astype(jnp.bfloat16)
    )
    hidden = hidden + jnp.dot(mixed, cell_merge, preferred_element_type=jnp.float32)
    normed = normalize(hidden, gain_layers).astype(jnp.bfloat16)
    layer_factor = layer_scale / math.sqrt(HDIM)
    proj = jnp.dot(normed, layer_heads, preferred_element_type=jnp.float32)
    layer_queries = head_norm(proj[..., :width]).astype(jnp.bfloat16)
    layer_keys = head_norm(proj[..., width : 2 * width]).astype(jnp.bfloat16)
    layer_values = split_heads(proj[..., 2 * width :])
    layer_ids = layer_first + jnp.arange(lay_count)
    start_layers = (
        jnp.full((shw_count, cell_count, HEADS, lay_count), -1e30, jnp.float32),
        jnp.zeros((shw_count, cell_count, HEADS, lay_count), jnp.float32),
        jnp.zeros((shw_count, cell_count, HEADS, lay_count, HDIM), jnp.float32),
    )
    pieces = (
        lax.all_gather(layer_keys, "layer", axis=1, tiled=True),
        lax.all_gather(layer_values, "layer", axis=1, tiled=True),
    )
    count = pieces[0].shape[1]
    scores = (
        jnp.einsum(
            "sqchd,skchd->schqk", layer_queries, pieces[0], preferred_element_type=jnp.float32
        )
        * layer_factor[None, None, :, None, None]
    )
    key_ok = layer_valid == 1
    allowed = key_ok[None, :] | (jnp.arange(count)[None, :] == layer_ids[:, None])
    carry = online(start_layers, scores, allowed[None, None, None], pieces[1], "schqk,skchd->schqd")
    result = carry[2] / carry[1][..., None]
    mixed = (
        jnp.transpose(result, (0, 3, 1, 2, 4))
        .reshape(shw_count, lay_count, cell_count, width)
        .astype(jnp.bfloat16)
    )
    hidden = hidden + jnp.dot(mixed, layer_merge, preferred_element_type=jnp.float32)
    normed = normalize(hidden, gain_expand).astype(jnp.bfloat16)
    inner = jax.nn.gelu(jnp.dot(normed, expand_weight, preferred_element_type=jnp.float32)).astype(
        jnp.bfloat16
    )
    hidden = hidden + jnp.dot(inner, reduce_weight, preferred_element_type=jnp.float32)
    velocity = jnp.sum(normalize(hidden, gain_final) * velocity_head, -1)
    velocity = (
        velocity
        * cell_ok[None, None, :].astype(jnp.float32)
        * layer_ok[None, :, None].astype(jnp.float32)
    )
    return (velocity, shower_state + velocity / STEPS)


def solution(mesh):
    return jax.shard_map(
        on_device,
        mesh=mesh,
        in_specs=(
            P(None, "layer", "cell"),
            P(),
            P(),
            P(),
            P(),
            P(),
            P("cell", None),
            P("layer", None),
            P(),
            P(),
            P(),
            P(),
            P(),
            P(),
            P(),
            P(),
            P(),
            P(),
            P(),
            P(),
            P(),
            P(),
        ),
        out_specs=(P(None, "layer", "cell"), P(None, "layer", "cell")),
        check_vma=False,
    )
```

profile of v0, /device:TPU:1, one launch (start us, length us, event | category | flops | bytes accessed | tf_op | source)
XLA Modules:
  0.0 406.8 jit_solution(17449303647220259367)
XLA Ops:
  7.2 0.9 iota_compare_fusion.2
  8.8 0.7 copy.68
  9.5 1.0 select_reduce_fusion
  10.5 1.1 multiply_reduce_fusion.8
  11.7 1.9 multiply_convert_fusion.8
  13.7 1.6 fusion.57
  15.3 1.5 reshape.228
  16.7 1.9 multiply_reduce_fusion.3
  18.8 0.1 copy.70
  19.0 1.9 multiply_convert_fusion.3
  20.9 89.2 %all-gather.4.cloned.1.call-done = bf16[2,6,1024,512]{3,2,1,0:T(8,128)(2,1)} async-done(((bf16[2,6,32,512]{3,2,1,0:T(8,128)(2,1)}), bf16[2,6,1024,512]{3,2,1,0:T(8,128)(2,1)}) %all-gather.4.cloned.1.call-update) | async-done | bytes 12582928 | tf_op jit(solution)/shard_map/all_gather | solution.py:99
  110.2 24.7 %fusion.43 = f32[2,6,1024,1024]{2,3,1,0:T(8,128)} fusion(bf16[2,6,1024,512]{3,2,1,0:T(8,128)(2,1)} %all-gather.4.cloned.1.call-done, bf16[512,1536]{1,0:T(8,128)(2,1)} %param.32), kind=kOutput, calls=%fused_computation.53 | convolution fusion | flops 12884901888 | bytes 63963136 | tf_op jit(solution)/shard_map/dot_general | solution.py:98
  134.8 13.4 %slice.46 = bf16[2,6,1024,512]{2,3,1,0:T(8,128)(2,1)} slice(f32[2,6,1024,1024]{2,3,1,0:T(8,128)} %fusion.43), slice={[0:2], [0:6], [0:1024], [512:1024]} | slice | bytes 25165824 | tf_op jit(solution)/shard_map/slice | solution.py:104
  148.2 17.5 %slice.30 = f32[2,6,1024,512]{2,3,1,0:T(8,128)} slice(f32[2,6,1024,1024]{2,3,1,0:T(8,128)} %fusion.43), slice={[0:2], [0:6], [0:1024], [0:512]} | slice | bytes 50331648 | tf_op jit(solution)/shard_map/slice | solution.py:103
  165.8 10.2 %multiply_reduce_fusion = f32[2,6,1024,8]{2,3,1,0:T(8,128)S(1)} fusion(f32[2,6,1024,1024]{2,3,1,0:T(8,128)} %fusion.43), kind=kLoop, calls=%fused_computation.2 | loop fusion | flops 12484608 | bytes 25559040 | tf_op jit(solution)/shard_map/reduce_sum | solution.py:22
  176.0 16.4 %fusion.2 = (f32[2,6,8,32]{3,2,1,0:T(8,128)S(1)}, f32[2,6,8,32,1024]{4,3,2,1,0:T(8,128)}) fusion(f32[8]{0:T(128)S(1)} %broadcast_multiply_fusion.1, pred[32,1024]{1,0:T(8,128)(4,1)S(1)} %fusion.66, f32[2,6,1024,8,64]{2,4,3,1,0:T(8,128)} %bitcast.78, f32[2,6,1024,8]{2,3,1,0:T(8,128)S(1)} %add_rsqrt_fusion, ...), kind=kOutput, calls=%fused_computation.7 | convolution fusion | flops 424670208 | bytes 38580256 | tf_op jit(solution)/shard_map/slqhd,slkhd->slhqk/dot_general | solution.py:107
  192.4 6.8 %fusion.3 = f32[2,6,8,32]{3,2,1,0:T(8,128)S(1)} fusion(f32[2,6,8,32,1024]{4,3,2,1,0:T(8,128)} %get-tuple-element.13, f32[2,6,8,32]{3,2,1,0:T(8,128)S(1)} %broadcast_maximum_fusion.1, f32[8]{0:T(128)S(1)} %broadcast_multiply_fusion.1, pred[32,1024]{1,0:T(8,128)(4,1)S(1)} %fusion.66), kind=kLoop, calls=%fused_computation.8 | loop fusion | flops 15725568 | bytes 12640288 | tf_op jit(solution)/shard_map/reduce_sum | solution.py:43
  199.2 14.3 %fusion.33 = bf16[2,6,32,8,64]{4,2,3,1,0:T(8,128)(2,1)} fusion(bf16[2,6,1024,8,64]{2,4,3,1,0:T(8,128)(2,1)} %bitcast.79, f32[2,6,8,32,1024]{4,3,2,1,0:T(8,128)} %get-tuple-element.13, f32[2,6,8,32]{3,2,1,0:T(8,128)S(1)} %broadcast_maximum_fusion.1, f32[8]{0:T(128)S(1)} %broadcast_multiply_fusion.1, pred[32,1024]{1,0:T(8,128)(4,1)S(1)} %fusion.66, ...), kind=kOutput, calls=%fused_computation.40 | convolution fusion | flops 418775040 | bytes 25616416 | tf_op jit(solution)/shard_map/slhqk,slkhd->slhqd/dot_general | solution.py:44
  213.6 1.5 copy.73
  215.0 0.5 convert_element_type.73
  215.5 1.6 multiply_reduce_fusion.7
  217.2 0.8 fusion.31
  218.0 1.4 copy-done.2
  219.4 1.0 fusion.78
  220.5 1.5 reshape.231
  221.9 1.9 multiply_reduce_fusion.1
  224.0 0.1 copy.77
  224.1 2.8 fusion.34
  227.0 1.2 slice.47
  228.1 0.4 convert_element_type.78
  228.5 1.0 copy.81
  229.8 2.6 reshape.230
  232.4 1.9 multiply_reduce_fusion.2
  234.4 0.1 copy.75
  234.5 1.9 multiply_convert_fusion.2
  236.4 70.1 %all-gather.6.cloned.1.call-done = bf16[2,48,32,8,64]{4,3,2,0,1:T(8,128)(2,1)} async-done(((bf16[2,6,32,8,64]{4,3,2,0,1:T(8,128)(2,1)}), bf16[2,48,32,8,64]{4,3,2,0,1:T(8,128)(2,1)}) %all-gather.6.cloned.1.call-update) | async-done | bytes 3145744 | tf_op jit(solution)/shard_map/all_gather | solution.py:133
  306.5 8.8 %fusion.28 = (f32[2,32,8,6]{3,2,1,0:T(8,128)S(1)}, f32[2,32,8,6,48]{4,3,2,1,0:T(8,128)S(1)}) fusion(f32[8]{0:T(128)S(1)} %broadcast_multiply_fusion, pred[6,48]{1,0:T(8,128)(4,1)S(1)} %fusion.67, bf16[2,48,32,8,64]{4,3,2,0,1:T(8,128)(2,1)} %all-gather.6.cloned.1.call-done, bf16[2,6,32,8,64]{4,3,2,1,0:T(8,128)(2,1)S(1)} %multiply_convert_fusion.2), kind=kOutput, calls=%fused_computation.36 | convolution fusion | flops 19313664 | bytes 4141376 | tf_op jit(solution)/shard_map/sqchd,skchd->schqk/dot_general | solution.py:138
  315.3 1.3 copy-done.1
  316.6 1.5 fusion.37
  318.2 63.8 %all-gather.8.cloned.1.call-done = bf16[2,48,32,8,64]{4,3,2,0,1:T(8,128)(2,1)} async-done(((bf16[2,6,32,8,64]{4,3,2,0,1:T(8,128)(2,1)}), bf16[2,48,32,8,64]{4,3,2,0,1:T(8,128)(2,1)}) %all-gather.8.cloned.1.call-update) | async-done | bytes 3145744 | tf_op jit(solution)/shard_map/all_gather | solution.py:134
  382.0 8.7 %fusion.27 = bf16[2,6,32,8,64]{4,1,3,2,0:T(8,128)(2,1)S(1)} fusion(bf16[2,48,32,8,64]{4,3,2,0,1:T(8,128)(2,1)} %all-gather.8.cloned.1.call-done, f32[2,32,8,6,48]{4,3,2,1,0:T(8,128)} %copy-done.1, f32[2,6,32,8]{1,3,2,0:T(8,128)S(1)} %bitcast.80, f32[2,32,8,6]{3,2,1,0:T(8,128)S(1)} %broadcast_maximum_fusion, f32[8]{0:T(128)S(1)} %broadcast_multiply_fusion, ...), kind=kOutput, calls=%fused_computation.33 | convolution fusion | flops 20004864 | bytes 4153664 | tf_op jit(solution)/shard_map/schqk,skchd->schqd/dot_general | solution.py:44
  390.6 0.1 copy.83
  390.8 0.5 convert_element_type.80
  391.2 1.7 multiply_reduce_fusion.6
  393.1 4.5 %multiply_reduce_fusion.5 = (f32[2,6,32]{2,1,0:T(8,128)S(1)}, f32[2,6,32,512]{3,2,1,0:T(8,128)}) fusion(f32[2,6,32,512]{3,2,1,0:T(8,128)S(1)} %get-tuple-element.19, bf16[2048,512]{1,0:T(8,128)(2,1)S(1)} %copy-done, bf16[512,2048]{1,0:T(8,128)(2,1)} %param.40, f32[512]{0:T(512)S(1)} %copy-done.13, f32[2,6,32]{2,1,0:T(8,128)S(1)} %add_rsqrt_fusion.5), kind=kOutput, calls=%fused_computation.65 | convolution fusion | flops 1618869888 | bytes 5772288 | tf_op jit(solution)/shard_map/dot_general | solution.py:157
  397.6 1.4 multiply_reduce_fusion.4
  399.1 0.6 copy.85
  399.7 0.6 copy.86
  (65 shorter events, 1.2 us)
Async XLA Ops:
  7.2 385.8 %copy-start = (bf16[2048,512]{1,0:T(8,128)(2,1)S(1)}, bf16[2048,512]{1,0:T(8,128)(2,1)}, u32[]{:S(2)}) copy-start(bf16[2048,512]{1,0:T(8,128)(2,1)} %param.41) | copy-start | bytes 6291460
  7.2 103.0 %all-gather.4.cloned.1.call-start = ((), (), s32[]{:S(2)}) async-start(), calls=%async_computation | async-start | bytes 12976128 | tf_op jit(solution)/shard_map/all_gather | solution.py:99
  13.6 292.9 %all-gather.6.cloned.1.call-start = ((), (), s32[]{:S(2)}) async-start(), calls=%async_computation.1 | async-start | bytes 7077888 | tf_op jit(solution)/shard_map/all_gather | solution.py:133
  13.6 5.3 %copy-start.14 = (f32[8]{0:T(128)S(1)}, f32[8]{0:T(128)}, u32[]{:S(2)}) copy-start(f32[8]{0:T(128)} %param.34) | copy-start | bytes 100
  13.7 5.3 %copy-start.10 = (s32[1024]{0:T(1024)S(1)}, s32[1024]{0:T(1024)}, u32[]{:S(2)}) copy-start(s32[1024]{0:T(1024)} %param.23) | copy-start | bytes 12292
  199.2 16.3 %copy-start.5 = (f32[32,512]{1,0:T(8,128)S(1)}, f32[32,512]{1,0:T(8,128)}, u32[]{:S(2)}) copy-start(f32[32,512]{1,0:T(8,128)} %param.28) | copy-start | bytes 196612
  199.2 16.3 %copy-start.6 = (f32[6,512]{1,0:T(8,128)S(1)}, f32[6,512]{1,0:T(8,128)}, u32[]{:S(2)}) copy-start(f32[6,512]{1,0:T(8,128)} %param.29) | copy-start | bytes 36868
  199.2 16.3 %copy-start.8 = (f32[512]{0:T(512)S(1)}, f32[512]{0:T(512)}, u32[]{:S(2)}) copy-start(f32[512]{0:T(512)} %param.27) | copy-start | bytes 6148
  213.6 3.6 copy-start.9
  215.5 1.7 copy-start.4
  217.2 3.3 copy-start.3
  218.0 1.4 copy-start.2
  226.9 2.8 copy-start.15
  226.9 2.8 copy-start.16
  226.9 155.0 %all-gather.8.cloned.1.call-start = ((), (), s32[]{:S(2)}) async-start(), calls=%async_computation.2 | async-start | bytes 7077888 | tf_op jit(solution)/shard_map/all_gather | solution.py:134
  315.3 1.4 copy-start.1
  390.6 2.4 copy-start.13
  393.0 4.6 %copy-start.11 = (f32[512]{0:T(512)S(1)}, f32[512]{0:T(512)}, u32[]{:S(2)}) copy-start(f32[512]{0:T(512)} %param.43) | copy-start | bytes 6148
  393.0 4.6 %copy-start.12 = (f32[512]{0:T(512)S(1)}, f32[512]{0:T(512)}, u32[]{:S(2)}) copy-start(f32[512]{0:T(512)} %param.42) | copy-start | bytes 6148
  393.0 6.0 %copy-start.7 = (f32[2,6,32]{2,0,1:T(2,128)S(1)}, f32[2,6,32]{2,0,1:T(2,128)}, u32[]{:S(2)}) copy-start(f32[2,6,32]{2,0,1:T(2,128)} %param.22) | copy-start | bytes 4612
Sparse Core Ops, SparseCore 0:
  13.7 96.4 all-gather.3
  227.0 79.4 all-gather.5
  308.3 73.6 all-gather.7
where the time goes:
time: 408 us; the launch traced here: 407 us
  waiting for transfers between devices  223 us (55%)
  matrix products  83.2 us (20%)
  local copies, waits for them, and re-layouts  47.8 us (12%)
  other arithmetic  37.7 us (9%)
  between operations  14.9 us (4%)
    all_gather x1, waiting for transfers between devices, on_device(): lax.all_gather(normed, 'cell', axis=2, tiled=True)  89.2 us
    all_gather x1, waiting for transfers between devices, on_device(): lax.all_gather(layer_keys, 'layer', axis=1, tiled=True)  70.1 us
    all_gather x1, waiting for transfers between devices, on_device(): lax.all_gather(layer_values, 'layer', axis=1, tiled=True)  63.8 us
    dot_general x1, matrix products, on_device(): jnp.dot(lax.all_gather(normed, 'cell', axis=2, tiled=True), cell_heads[:,...  24.7 us
    dot_general x2, matrix products, online(): jnp.einsum(form, weights.astype(jnp.bfloat16), values, preferred_element_...  23 us
    slice x1, local copies, waits for them, and re-layouts, on_device(): keys = head_norm(proj[..., :width]).astype(jnp.bfloat16)  17.5 us
    dot_general x1, matrix products, on_device(): jnp.einsum('slqhd,slkhd->slhqk', queries, keys, preferred_element_type=jn...  16.4 us
    reduce_sum x4, other arithmetic, head_norm(): return split * lax.rsqrt(jnp.mean(split * split, -1, keepdims=True) + EPS)  15.9 us
  transfers between devices with their start and end apart: 3, of which 3 were waited for; matrix products, arithmetic and copies ran while one was open for 7% of the time, Pallas kernels for 0%

commit v1 on v0

--- a/solution.py
+++ b/solution.py
@@ -131,7 +131,15 @@
     )
     pieces = (
         lax.all_gather(layer_keys, "layer", axis=1, tiled=True),
-        lax.all_gather(layer_values, "layer", axis=1, tiled=True),
+        jnp.concatenate(
+            lax.all_to_all(
+                jnp.stack([layer_values for _ in range(lax.axis_size("layer"))], axis=0),
+                "layer",
+                0,
+                0,
+            ),
+            axis=1,
+        ),
     )
     count = pieces[0].shape[1]
     scores = (

time: 408 us -> 381 us (0.934)
  waiting for transfers between devices: 223 us -> 161 us
  local copies, waits for them, and re-layouts: 47.8 us -> 70.6 us
  starting transfers between devices: 0.12 us -> 10.8 us
    all_gather x1 -> x0, waiting for transfers between devices: 63.8 us -> none  [on_device(): lax.all_gather(layer_values, 'layer', axis=1, tiled=True)]
    all_to_all x0 -> x1, waiting for transfers between devices: none -> 40.7 us  [on_device(): lax.all_to_all(jnp.stack([layer_values for _ in range(lax.axis_size('laye...]
    all_gather x1, waiting for transfers between devices: 70.1 us -> 30.5 us  [on_device(): lax.all_gather(layer_keys, 'layer', axis=1, tiled=True)]
    unnamed x37 -> x41, local copies, waits for them, and re-layouts: 4.71 us -> 19.8 us
    all_to_all x0 -> x1, starting transfers between devices: none -> 10.7 us  [on_device(): lax.all_to_all(jnp.stack([layer_values for _ in range(lax.axis_size('laye...]
    all_to_all x0 -> x1, local copies, waits for them, and re-layouts: none -> 6.3 us  [on_device(): lax.all_to_all(jnp.stack([layer_values for _ in range(lax.axis_size('laye...]
    another operation x0 -> x1, local copies, waits for them, and re-layouts: none -> 4.21 us  [on_device(): jnp.stack([layer_values for _ in range(lax.axis_size('layer'))], axis=0)]
  transfers between devices with their start and end apart: 3 -> 3, of which waited for: 3 -> 3; matrix products, arithmetic and copies ran while one was open for 7% -> 9% of each run, Pallas kernels for 0% -> 0%
where the time goes in v1:
time: 381 us; the launch traced here: 380 us
  waiting for transfers between devices  161 us (42%)
  matrix products  85.4 us (22%)
  local copies, waits for them, and re-layouts  70.6 us (19%)
  other arithmetic  37.5 us (10%)
  between operations  15.2 us (4%)
  starting transfers between devices  10.8 us (3%)
    all_gather x1, waiting for transfers between devices, on_device(): lax.all_gather(normed, 'cell', axis=2, tiled=True)  89.3 us
    all_to_all x1, waiting for transfers between devices, on_device(): lax.all_to_all(jnp.stack([layer_values for _ in range(lax.axis_size('laye...  40.7 us
    all_gather x1, waiting for transfers between devices, on_device(): lax.all_gather(layer_keys, 'layer', axis=1, tiled=True)  30.5 us
    dot_general x2, matrix products, online(): jnp.einsum(form, weights.astype(jnp.bfloat16), values, preferred_element_...  25.1 us
    dot_general x1, matrix products, on_device(): jnp.dot(lax.all_gather(normed, 'cell', axis=2, tiled=True), cell_heads[:,...  24.7 us
    unnamed x41, local copies, waits for them, and re-layouts  19.8 us
    slice x1, local copies, waits for them, and re-layouts, on_device(): keys = head_norm(proj[..., :width]).astype(jnp.bfloat16)  17.5 us
    dot_general x1, matrix products, on_device(): jnp.einsum('slqhd,slkhd->slhqk', queries, keys, preferred_element_type=jn...  16.4 us
  transfers between devices with their start and end apart: 3, of which 3 were waited for; matrix products, arithmetic and copies ran while one was open for 9% of the time, Pallas kernels for 0%

profile of v1, /device:TPU:1, one launch (start us, length us, event | category | flops | bytes accessed | tf_op | source)
XLA Modules:
  0.0 380.0 jit_solution(28393359245512313)
XLA Ops:
  7.2 0.9 iota_compare_fusion.2
  8.8 0.7 copy.68
  9.5 1.0 select_reduce_fusion
  10.5 1.1 multiply_reduce_fusion.8
  11.7 1.9 multiply_convert_fusion.8
  13.6 1.6 fusion.57
  15.2 1.5 reshape.237
  16.7 1.9 multiply_reduce_fusion.3
  18.7 0.1 copy.70
  19.0 1.9 multiply_convert_fusion.3
  20.9 89.3 %all-gather.3.cloned.1.call-done = bf16[2,6,1024,512]{3,2,1,0:T(8,128)(2,1)} async-done(((bf16[2,6,32,512]{3,2,1,0:T(8,128)(2,1)}), bf16[2,6,1024,512]{3,2,1,0:T(8,128)(2,1)}) %all-gather.3.cloned.1.call-update) | async-done | bytes 12582928 | tf_op jit(solution)/shard_map/all_gather | solution.py:99
  110.2 24.7 %fusion.43 = f32[2,6,1024,1024]{2,3,1,0:T(8,128)} fusion(bf16[2,6,1024,512]{3,2,1,0:T(8,128)(2,1)} %all-gather.3.cloned.1.call-done, bf16[512,1536]{1,0:T(8,128)(2,1)} %param.32), kind=kOutput, calls=%fused_computation.53 | convolution fusion | flops 12884901888 | bytes 63963136 | tf_op jit(solution)/shard_map/dot_general | solution.py:98
  134.8 13.4 %slice.46 = bf16[2,6,1024,512]{2,3,1,0:T(8,128)(2,1)} slice(f32[2,6,1024,1024]{2,3,1,0:T(8,128)} %fusion.43), slice={[0:2], [0:6], [0:1024], [512:1024]} | slice | bytes 25165824 | tf_op jit(solution)/shard_map/slice | solution.py:104
  148.2 17.5 %slice.30 = f32[2,6,1024,512]{2,3,1,0:T(8,128)} slice(f32[2,6,1024,1024]{2,3,1,0:T(8,128)} %fusion.43), slice={[0:2], [0:6], [0:1024], [0:512]} | slice | bytes 50331648 | tf_op jit(solution)/shard_map/slice | solution.py:103
  165.8 10.2 %multiply_reduce_fusion = f32[2,6,1024,8]{2,3,1,0:T(8,128)S(1)} fusion(f32[2,6,1024,1024]{2,3,1,0:T(8,128)} %fusion.43), kind=kLoop, calls=%fused_computation.2 | loop fusion | flops 12484608 | bytes 25559040 | tf_op jit(solution)/shard_map/reduce_sum | solution.py:22
  176.1 16.4 %fusion.2 = (f32[2,6,8,32]{3,2,1,0:T(8,128)S(1)}, f32[2,6,8,32,1024]{4,3,2,1,0:T(8,128)}) fusion(f32[8]{0:T(128)S(1)} %broadcast_multiply_fusion.1, pred[32,1024]{1,0:T(8,128)(4,1)S(1)} %fusion.66, f32[2,6,1024,8,64]{2,4,3,1,0:T(8,128)} %bitcast.81, f32[2,6,1024,8]{2,3,1,0:T(8,128)S(1)} %add_rsqrt_fusion, ...), kind=kOutput, calls=%fused_computation.7 | convolution fusion | flops 424670208 | bytes 38580256 | tf_op jit(solution)/shard_map/slqhd,slkhd->slhqk/dot_general | solution.py:107
  192.4 6.8 %fusion.3 = f32[2,6,8,32]{3,2,1,0:T(8,128)S(1)} fusion(f32[2,6,8,32,1024]{4,3,2,1,0:T(8,128)} %get-tuple-element.13, f32[2,6,8,32]{3,2,1,0:T(8,128)S(1)} %broadcast_maximum_fusion.1, f32[8]{0:T(128)S(1)} %broadcast_multiply_fusion.1, pred[32,1024]{1,0:T(8,128)(4,1)S(1)} %fusion.66), kind=kLoop, calls=%fused_computation.8 | loop fusion | flops 15725568 | bytes 12640288 | tf_op jit(solution)/shard_map/reduce_sum | solution.py:43
  199.2 14.4 %fusion.33 = bf16[2,6,32,8,64]{4,2,3,1,0:T(8,128)(2,1)} fusion(bf16[2,6,1024,8,64]{2,4,3,1,0:T(8,128)(2,1)} %bitcast.82, f32[2,6,8,32,1024]{4,3,2,1,0:T(8,128)} %get-tuple-element.13, f32[2,6,8,32]{3,2,1,0:T(8,128)S(1)} %broadcast_maximum_fusion.1, f32[8]{0:T(128)S(1)} %broadcast_multiply_fusion.1, pred[32,1024]{1,0:T(8,128)(4,1)S(1)} %fusion.66, ...), kind=kOutput, calls=%fused_computation.40 | convolution fusion | flops 418775040 | bytes 25616416 | tf_op jit(solution)/shard_map/slhqk,slkhd->slhqd/dot_general | solution.py:44
  213.6 1.5 copy.73
  215.1 0.5 convert_element_type.75
  215.6 1.6 multiply_reduce_fusion.7
  217.2 0.8 fusion.31
  218.1 1.4 fusion.78
  219.5 0.4 convert_element_type.80
  219.9 4.2 %stack.2 = bf16[8,2,6,32,8,64]{5,4,3,2,1,0:T(8,128)(2,1)} broadcast(bf16[2,6,32,8,64]{4,3,2,1,0:T(8,128)(2,1)S(1)} %convert_element_type.80), dimensions={1,2,3,4,5} | broadcast | bytes 3538944 | tf_op jit(solution)/shard_map/stack | solution.py:136
  224.1 8.9 %reshape.250 = bf16[8,2,98304]{2,1,0:T(2,128)(2,1)} reshape(bf16[8,2,6,32,8,64]{5,4,3,2,1,0:T(8,128)(2,1)} %stack.2) | data formatting | bytes 6291456
  233.0 10.7 %all-to-all-start = ((bf16[8,2,98304]{2,1,0:T(2,128)(2,1)}), bf16[8,2,98304]{2,1,0:T(2,128)(2,1)}, u32[]{:S(2)}, u32[]{:S(2)}) async-start(bf16[8,2,98304]{2,1,0:T(2,128)(2,1)} %reshape.250), calls=%async_computation | async-start | bytes 6291456 | tf_op jit(solution)/shard_map/all_to_all | solution.py:135
  243.8 1.5 reshape.240
  245.3 2.0 multiply_reduce_fusion.1
  247.4 0.1 copy.77
  247.5 2.8 fusion.34
  250.6 1.5 reshape.239
  252.1 1.9 multiply_reduce_fusion.2
  254.2 1.9 multiply_convert_fusion.2
  256.1 40.7 %all-to-all-done = bf16[8,2,98304]{2,1,0:T(2,128)(2,1)} async-done(((bf16[8,2,98304]{2,1,0:T(2,128)(2,1)}), bf16[8,2,98304]{2,1,0:T(2,128)(2,1)}, u32[]{:S(2)}, u32[]{:S(2)}) %all-to-all-start) | async-done | bytes 3145760 | tf_op jit(solution)/shard_map/all_to_all | solution.py:135
  296.9 8.8 %reshape.251 = bf16[8,2,6,32,8,64]{5,4,3,2,1,0:T(8,128)(2,1)} reshape(bf16[8,2,98304]{2,1,0:T(2,128)(2,1)} %all-to-all-done) | data formatting | bytes 6291456
  305.7 6.3 %copy.81 = bf16[8,2,6,32,8,64]{5,4,3,2,0,1:T(8,128)(2,1)} copy(bf16[8,2,6,32,8,64]{5,4,3,2,1,0:T(8,128)(2,1)} %reshape.251) | data formatting | bytes 6291456 | tf_op jit(solution)/shard_map/all_to_all | solution.py:135
  312.0 30.5 %all-gather.5.cloned.1.call-done = bf16[2,48,32,8,64]{4,3,2,0,1:T(8,128)(2,1)} async-done(((bf16[2,6,32,8,64]{4,3,2,0,1:T(8,128)(2,1)}), bf16[2,48,32,8,64]{4,3,2,0,1:T(8,128)(2,1)}) %all-gather.5.cloned.1.call-update) | async-done | bytes 3145744 | tf_op jit(solution)/shard_map/all_gather | solution.py:133
  342.5 8.9 %fusion.28 = (f32[2,32,8,6]{3,2,1,0:T(8,128)S(1)}, f32[2,32,8,6,48]{4,3,2,1,0:T(8,128)S(1)}) fusion(f32[8]{0:T(128)S(1)} %broadcast_multiply_fusion, pred[6,48]{1,0:T(8,128)(4,1)S(1)} %fusion.67, bf16[2,48,32,8,64]{4,3,2,0,1:T(8,128)(2,1)} %all-gather.5.cloned.1.call-done, bf16[2,6,32,8,64]{4,3,2,1,0:T(8,128)(2,1)S(1)} %multiply_convert_fusion.2), kind=kOutput, calls=%fused_computation.36 | convolution fusion | flops 19313664 | bytes 4141376 | tf_op jit(solution)/shard_map/sqchd,skchd->schqk/dot_general | solution.py:146
  351.4 1.3 fusion.37
  352.8 10.8 %fusion.27 = bf16[2,6,32,8,64]{4,1,3,2,0:T(8,128)(2,1)S(1)} fusion(bf16[2,48,32,8,64]{4,3,2,1,0:T(8,128)(2,1)S(1)} %bitcast.83, f32[2,32,8,6,48]{4,3,2,1,0:T(8,128)S(1)} %get-tuple-element.17, f32[2,6,32,8]{1,3,2,0:T(8,128)S(1)} %bitcast.84, f32[2,32,8,6]{3,2,1,0:T(8,128)S(1)} %broadcast_maximum_fusion, f32[8]{0:T(128)S(1)} %broadcast_multiply_fusion, ...), kind=kOutput, calls=%fused_computation.33 | convolution fusion | flops 20004864 | bytes 4153664 | tf_op jit(solution)/shard_map/schqk,skchd->schqd/dot_general | solution.py:44
  363.5 0.1 copy.83
  363.7 0.5 convert_element_type.82
  364.1 1.7 multiply_reduce_fusion.6
  366.0 4.5 %multiply_reduce_fusion.5 = (f32[2,6,32]{2,1,0:T(8,128)S(1)}, f32[2,6,32,512]{3,2,1,0:T(8,128)}) fusion(f32[2,6,32,512]{3,2,1,0:T(8,128)S(1)} %get-tuple-element.19, bf16[2048,512]{1,0:T(8,128)(2,1)S(1)} %copy-done, bf16[512,2048]{1,0:T(8,128)(2,1)} %param.40, f32[512]{0:T(512)S(1)} %copy-done.14, f32[2,6,32]{2,1,0:T(8,128)S(1)} %add_rsqrt_fusion.5), kind=kOutput, calls=%fused_computation.65 | convolution fusion | flops 1618869888 | bytes 5772288 | tf_op jit(solution)/shard_map/dot_general | solution.py:165
  370.5 1.4 multiply_reduce_fusion.4
  372.0 0.6 copy.85
  372.6 0.6 copy.86
  (69 shorter events, 1.3 us)
Async XLA Ops:
  7.2 358.7 %copy-start = (bf16[2048,512]{1,0:T(8,128)(2,1)S(1)}, bf16[2048,512]{1,0:T(8,128)(2,1)}, u32[]{:S(2)}) copy-start(bf16[2048,512]{1,0:T(8,128)(2,1)} %param.41) | copy-start | bytes 6291460
  7.2 103.0 %all-gather.3.cloned.1.call-start = ((), (), s32[]{:S(2)}) async-start(), calls=%async_computation.1 | async-start | bytes 12976128 | tf_op jit(solution)/shard_map/all_gather | solution.py:99
  13.6 5.3 %copy-start.15 = (f32[8]{0:T(128)S(1)}, f32[8]{0:T(128)}, u32[]{:S(2)}) copy-start(f32[8]{0:T(128)} %param.34) | copy-start | bytes 100
  13.6 5.3 %copy-start.11 = (s32[1024]{0:T(1024)S(1)}, s32[1024]{0:T(1024)}, u32[]{:S(2)}) copy-start(s32[1024]{0:T(1024)} %param.23) | copy-start | bytes 12292
  199.2 16.3 %copy-start.6 = (f32[32,512]{1,0:T(8,128)S(1)}, f32[32,512]{1,0:T(8,128)}, u32[]{:S(2)}) copy-start(f32[32,512]{1,0:T(8,128)} %param.28) | copy-start | bytes 196612
  199.2 16.3 %copy-start.7 = (f32[6,512]{1,0:T(8,128)S(1)}, f32[6,512]{1,0:T(8,128)}, u32[]{:S(2)}) copy-start(f32[6,512]{1,0:T(8,128)} %param.29) | copy-start | bytes 36868
  199.2 16.3 %copy-start.9 = (f32[512]{0:T(512)S(1)}, f32[512]{0:T(512)}, u32[]{:S(2)}) copy-start(f32[512]{0:T(512)} %param.27) | copy-start | bytes 6148
  213.6 3.6 copy-start.10
  215.6 1.7 copy-start.5
  217.2 0.9 copy-start.2
  233.0 10.8 %copy-start.4 = (f32[2,6,32,512]{3,2,1,0:T(8,128)S(1)}, f32[2,6,32,512]{3,2,1,0:T(8,128)}, u32[]{:S(2)}) copy-start(f32[2,6,32,512]{3,2,1,0:T(8,128)} %get-tuple-element.11) | copy-start | bytes 2359300
  233.0 63.8 %all-to-all-start = ((bf16[8,2,98304]{2,1,0:T(2,128)(2,1)}), bf16[8,2,98304]{2,1,0:T(2,128)(2,1)}, u32[]{:S(2)}, u32[]{:S(2)}) async-start(bf16[8,2,98304]{2,1,0:T(2,128)(2,1)} %reshape.250), calls=%async_computation | async-start | bytes 6291456 | tf_op jit(solution)/shard_map/all_to_all | solution.py:135
  243.8 98.7 %all-gather.5.cloned.1.call-start = ((), (), s32[]{:S(2)}) async-start(), calls=%async_computation.2 | async-start | bytes 7077888 | tf_op jit(solution)/shard_map/all_gather | solution.py:133
  245.3 5.1 %copy-start.16 = (s32[48]{0:T(128)S(1)}, s32[48]{0:T(128)}, u32[]{:S(2)}) copy-start(s32[48]{0:T(128)} %param.24) | copy-start | bytes 580
  245.3 5.2 %copy-start.17 = (f32[8]{0:T(128)S(1)}, f32[8]{0:T(128)}, u32[]{:S(2)}) copy-start(f32[8]{0:T(128)} %param.38) | copy-start | bytes 100
  245.3 5.3 %copy-start.3 = (f32[2,6,32,512]{3,2,1,0:T(8,128)S(1)}, f32[2,6,32,512]{3,2,1,0:T(8,128)}, u32[]{:S(2)}) copy-start(f32[2,6,32,512]{3,2,1,0:T(8,128)} %get-tuple-element.10) | copy-start | bytes 2359300
  342.5 10.3 %copy-start.1 = (bf16[8,2,6,32,8,64]{5,4,3,2,0,1:T(8,128)(2,1)S(1)}, bf16[8,2,6,32,8,64]{5,4,3,2,0,1:T(8,128)(2,1)}, u32[]{:S(2)}) copy-start(bf16[8,2,6,32,8,64]{5,4,3,2,0,1:T(8,128)(2,1)} %copy.81) | copy-start | bytes 9437188
  363.5 2.4 copy-start.14
  365.9 4.6 %copy-start.12 = (f32[512]{0:T(512)S(1)}, f32[512]{0:T(512)}, u32[]{:S(2)}) copy-start(f32[512]{0:T(512)} %param.43) | copy-start | bytes 6148
  365.9 4.6 %copy-start.13 = (f32[512]{0:T(512)S(1)}, f32[512]{0:T(512)}, u32[]{:S(2)}) copy-start(f32[512]{0:T(512)} %param.42) | copy-start | bytes 6148
  365.9 5.9 %copy-start.8 = (f32[2,6,32]{2,0,1:T(2,128)S(1)}, f32[2,6,32]{2,0,1:T(2,128)}, u32[]{:S(2)}) copy-start(f32[2,6,32]{2,0,1:T(2,128)} %param.22) | copy-start | bytes 4612
Sparse Core Ops, SparseCore 0:
  13.7 96.4 all-gather.2
  250.4 92.0 all-gather.4
